TPU v7x, 32 devices: a whole 2x2x4 slice. The times are simulated.
32 devices in a mesh: section: 4 (over x, core), shard: 4 (over z), replica: 2 (over y).
Axes of the slice: x: 2, y: 2, z: 4, core: 2. Of those that a mesh axis runs over, the one named last changes fastest.
Arguments:
- normed: bfloat16 [4, 2, 1024, 4096], P('section', None, ('shard', 'replica')), may hold values from -0.125 to 0.125
- key_cotangent: bfloat16 [4, 2, 1024, 512], P('section', None, ('shard', 'replica')), may hold values from -12 to 12
- positions: int32 [2, 1024], P(None, ('shard', 'replica')), may hold values from 0 to 1023, as said below
- key_weight: bfloat16 [4, 4096, 512], P('section', 'shard'), may hold values from -0.09375 to 0.09375
Outputs:
- key_weight_grad: bfloat16 [4, 4096, 512], P('section', 'shard')
- passed_grad: bfloat16 [4, 2, 1024, 4096], P('section', None, ('shard', 'replica'))
Inputs may be any that keep to these rules, and one draw needn't show every extreme that they name: `positions`: each token's position within its document of the micro-batch; in every micro-batch a document begins at every multiple of 1024 tokens, and in all but the first micro-batch at further places drawn at random.
All inputs are finite; a program needn't handle non-finite values.
Results may differ from a plain program's by a relative error of at most 0.018.
Values may be sent and summed in bfloat16 or wider, within the bound.
No kernel may reach another device: no remote copies, remote signals or barrier semaphores. Data moves between devices by JAX's collectives and lax.ppermute only.
A program may use at most 64 MiB of HBM per device.

v0:
```python
import jax
import jax.numpy as jnp
from jax import lax
from jax.sharding import PartitionSpec as P

HEAD = 128


def shifted(value, axis, steps):
    count = lax.axis_size(axis)
    leading, last = (max(0, -steps), min(count, count - steps))
    return lax.ppermute(value, axis, [(source, source + steps) for source in range(leading, last)])


def undo_rotation(cotangent, positions):
    half = HEAD // 2
    heads = cotangent.shape[-1] // HEAD
    index = jnp.arange(half, dtype=jnp.float32)
    freq = jnp.power(jnp.float32(500000.0), -2.0 * index / HEAD)
    angle = positions.astype(jnp.float32)[..., None] * freq
    angle = jnp.concatenate([angle, angle], axis=-1)[:, :, None, :]
    cosine = jnp.cos(angle)
    sine = jnp.sin(angle)
    lead = cotangent.shape[:2]
    grads = cotangent.astype(jnp.float32).reshape(lead + (heads, HEAD))
    swapped = jnp.concatenate([grads[..., half:], -grads[..., :half]], axis=-1)
    result = grads * cosine + swapped * sine
    return result.reshape(lead + (heads * HEAD,)).astype(jnp.bfloat16)


def per_device(normed, key_cotangent, positions, key_weight):
    key_grad = undo_rotation(key_cotangent[0], positions)
    width = normed.shape[3]
    local_rows = key_weight[0]
    partial_cols = jnp.einsum(
        "mtk,dk->mtd",
        lax.all_gather(key_grad, "shard", axis=1, tiled=True),
        local_rows,
        preferred_element_type=jnp.float32,
    ).astype(jnp.bfloat16)
    moved = lax.all_to_all(partial_cols, "shard", split_axis=1, concat_axis=2, tiled=True)
    input_grad = moved[:, :, :width][None]
    passed = shifted(input_grad, "section", -1)
    steps_tok = normed.shape[1] * normed.shape[2]
    flat_in = normed[0].reshape(steps_tok, width)
    flat_key = key_grad.reshape(steps_tok, key_grad.shape[-1])
    padding = lax.axis_size("shard") * local_rows.shape[0] - width
    padded = jnp.pad(flat_in, ((0, 0), (0, padding)))
    shard_total = lax.psum_scatter(
        lax.dot_general(
            padded, flat_key, (((0,), (0,)), ((), ())), preferred_element_type=jnp.float32
        ).astype(jnp.bfloat16),
        "shard",
        scatter_dimension=0,
        tiled=True,
    )
    shard_round = lax.optimization_barrier(shard_total).astype(jnp.float32)
    total = lax.psum(shard_round.astype(jnp.bfloat16), "replica")
    return (total[None], passed)


def solution(mesh):
    in_specs = (
        P("section", None, ("shard", "replica"), None),
        P("section", None, ("shard", "replica"), None),
        P(None, ("shard", "replica")),
        P("section", "shard", None),
    )
    out_specs = (P("section", "shard", None), P("section", None, ("shard", "replica"), None))
    return jax.shard_map(
        per_device, mesh=mesh, in_specs=in_specs, out_specs=out_specs, check_vma=False
    )
```

profile of v0, /device:TPU:0, one launch (start us, length us, event | category | flops | bytes accessed | tf_op | source)
XLA Modules:
  0.0 222.6 jit_solution(9915633863694696768)
XLA Ops:
  7.2 0.0 copy-start
  7.2 0.0 all-gather.2.cloned.1.call-start
  7.2 1.3 reshape.72
  8.5 0.7 convert_element_type.52
  9.2 0.1 broadcast_multiply_fusion
  9.3 0.5 fusion.6
  9.8 0.4 fusion.8
  10.2 0.5 add_convert_fusion
  10.7 0.2 mul.71
  10.9 0.9 mul.65
  11.8 1.3 mul.69
  13.0 1.8 fusion.3
  14.8 0.0 all-gather.2.cloned.1.call-update
  14.9 0.0 reduce-scatter.2.cloned.1.call-start
  14.9 0.0 copy-done
  14.9 3.2 %fusion = bf16[4096,512]{0,1:T(8,128)(2,1)} fusion(bf16[256,4096]{1,0:T(8,128)(2,1)S(1)} %bitcast.26, bf16[32,8,4,128]{3,2,1,0:T(4,128)(2,1)S(1)} %bitcast.28), kind=kOutput, calls=%fused_computation.1 | convolution fusion | flops 1075838976 | bytes 6553600 | tf_op jit(solution)/shard_map/dot_general | solution.py:50
  18.2 0.0 copy-start.1
  18.2 0.0 reduce-scatter.2.cloned.1.call-update
  18.2 0.0 all-reduce.2.cloned.1.call-start
  18.2 27.5 %all-gather.2.cloned.1.call-done = bf16[2,512,512]{2,1,0:T(8,128)(2,1)} async-done(((bf16[2,128,512]{2,1,0:T(8,128)(2,1)}), bf16[2,512,512]{2,1,0:T(8,128)(2,1)}) %all-gather.2.cloned.1.call-update) | async-done | bytes 1048592 | tf_op jit(solution)/shard_map/all_gather | solution.py:37
  45.7 0.0 copy-done.1
  45.7 2.5 %convolution_convert_fusion.1 = bf16[2,512,1024]{2,1,0:T(8,128)(2,1)S(1)} fusion(bf16[2,512,512]{2,1,0:T(8,128)(2,1)} %all-gather.2.cloned.1.call-done, bf16[1,1024,512]{2,1,0:T(8,128)(2,1)S(1)} %copy-done.1), kind=kOutput, calls=%fused_computation.2 | convolution fusion | flops 1074790400 | bytes 4194304 | tf_op jit(solution)/shard_map/mtk,dk->mtd/dot_general | solution.py:35
  48.2 2.2 copy.8
  50.4 107.6 %all_to_all.15 = bf16[2,512,1024]{2,0,1:T(2,128)(2,1)S(1)} all-to-all(bf16[2,512,1024]{2,0,1:T(2,128)(2,1)S(1)} %copy.8), channel_id=1, replica_groups=mesh['section'=4,'shard'=4,'replica'=2] {'shard'}, dimensions={1} | all-to-all | bytes 4194304 | tf_op jit(solution)/shard_map/all_to_all | solution.py:41
  158.0 2.9 %copy.9 = bf16[2,128,4,1024]{3,2,1,0:T(4,128)(2,1)} copy(bf16[2,128,4,1024]{3,0,1,2:T(2,128)(2,1)S(1)} %bitcast.27) | data formatting | bytes 4194304 | tf_op jit(solution)/shard_map/all_to_all | solution.py:41
  161.0 4.5 %broadcast_in_dim.10 = bf16[1,2,128,4096]{3,2,1,0:T(8,128)(2,1)} reshape(bf16[2,128,4,1024]{3,2,1,0:T(4,128)(2,1)} %copy.9) | data formatting | bytes 4194304 | tf_op jit(solution)/shard_map/broadcast_in_dim | solution.py:42
  165.5 1.3 collective-permute-start
  166.8 0.0 reduce-scatter.2.cloned.1.call-done
  166.8 0.0 all-reduce.2.cloned.1.call-update
  166.9 5.0 %collective-permute-done = bf16[1,2,128,4096]{3,2,1,0:T(8,128)(2,1)} collective-permute-done((bf16[1,2,128,4096]{3,2,1,0:T(8,128)(2,1)}, bf16[1,2,128,4096]{3,2,1,0:T(8,128)(2,1)}, u32[]{:S(2)}, u32[]{:S(2)}) %collective-permute-start) | collective-permute-done | bytes 2097184 | tf_op jit(solution)/shard_map/ppermute | solution.py:12
  171.9 38.7 %all-reduce.2.cloned.1.call-done = bf16[1,1024,512]{1,2,0:T(8,128)(2,1)} async-done(((bf16[1,1024,512]{1,2,0:T(8,128)(2,1)}), bf16[1,1024,512]{1,2,0:T(8,128)(2,1)}) %all-reduce.2.cloned.1.call-update) | async-done | bytes 1048592 | tf_op jit(solution)/shard_map/psum | solution.py:58
  210.6 2.3 %copy.10 = bf16[1,1024,512]{2,1,0:T(8,128)(2,1)} copy(bf16[1,1024,512]{1,2,0:T(8,128)(2,1)} %all-reduce.2.cloned.1.call-done) | data formatting | bytes 2097152
  212.9 3.1 %copy.18 = bf16[1,2,128,4096]{3,2,1,0:T(8,128)(2,1)} copy(bf16[1,2,128,4096]{3,2,1,0:T(8,128)(2,1)} %collective-permute-done) | data formatting | bytes 4194304
  (1 shorter events, 0.0 us)
Async XLA Ops:
  7.2 7.7 %copy-start = (bf16[1,2,128,4096]{3,2,1,0:T(8,128)(2,1)S(1)}, bf16[1,2,128,4096]{3,2,1,0:T(8,128)(2,1)}, u32[]{:S(2)}) copy-start(bf16[1,2,128,4096]{3,2,1,0:T(8,128)(2,1)} %param.4) | copy-start | bytes 6291460
  7.2 38.5 %all-gather.2.cloned.1.call-start = ((), (), s32[]{:S(2)}) async-start(), calls=%async_computation.4 | async-start | bytes 1310720 | tf_op jit(solution)/shard_map/all_gather | solution.py:37
  14.9 152.0 %reduce-scatter.2.cloned.1.call-start = ((), (), s32[]{:S(2)}) async-start(), calls=%async_computation.2 | async-start | bytes 5242880 | tf_op jit(solution)/shard_map/reduce_scatter | solution.py:49
  18.2 27.6 %copy-start.1 = (bf16[1,1024,512]{2,1,0:T(8,128)(2,1)S(1)}, bf16[1,1024,512]{2,1,0:T(8,128)(2,1)}, u32[]{:S(2)}) copy-start(bf16[1,1024,512]{2,1,0:T(8,128)(2,1)} %param.7) | copy-start | bytes 3145732
  18.2 192.5 %all-reduce.2.cloned.1.call-start = ((), (), s32[]{:S(2)}) async-start(), calls=%async_computation.3 | async-start | bytes 2097152 | tf_op jit(solution)/shard_map/psum | solution.py:58
  165.5 6.4 %collective-permute-start = (bf16[1,2,128,4096]{3,2,1,0:T(8,128)(2,1)}, bf16[1,2,128,4096]{3,2,1,0:T(8,128)(2,1)}, u32[]{:S(2)}, u32[]{:S(2)}) collective-permute-start(bf16[1,2,128,4096]{3,2,1,0:T(8,128)(2,1)} %broadcast_in_dim.10), channel_id=1, source_target_pairs={{8,0},{16,8},{24,16},{9,1},{17,9},{25,17},{10,2},{18,10},{26,18},{... | collective-permute-start | bytes 6291464 | tf_op jit(solution)/shard_map/ppermute | solution.py:12
Sparse Core Ops, SparseCore 0:
  15.0 30.6 all-gather.1
  48.0 115.0 reduce-scatter.1
  167.0 43.6 all-reduce.1
where the time goes:
time: 223 us
  blocking collectives  108 us (48%)
  waiting for transfers between devices  71.4 us (32%)
  local copies, waits for them, and re-layouts  18.6 us (8%)
  between operations  13.8 us (6%)
  matrix products  5.74 us (3%)
  other arithmetic  3.96 us (2%)
    all_to_all x1, blocking collectives, per_device(): lax.all_to_all(partial_cols, 'shard', split_axis=1, concat_axis=2, tiled=...  108 us
    psum x1, waiting for transfers between devices, per_device(): total = lax.psum(shard_round.astype(jnp.bfloat16), 'replica')  38.7 us
    all_gather x1, waiting for transfers between devices, per_device(): lax.all_gather(key_grad, 'shard', axis=1, tiled=True)  27.5 us
    unnamed x6, local copies, waits for them, and re-layouts  5.41 us
    ppermute x1, waiting for transfers between devices, shifted(): lax.ppermute(value, axis, [(source, source + steps) for source in range(l...  5.04 us
    broadcast_in_dim x1, local copies, waits for them, and re-layouts, per_device(): input_grad = moved[:, :, :width][None]  4.53 us
  transfers between devices with their start and end apart: 4, of which 3 were waited for; matrix products, arithmetic and copies ran while one was open for 7% of the time, Pallas kernels for 0%

commit v1 on v0

--- a/solution.py
+++ b/solution.py
@@ -4,6 +4,17 @@
 from jax.sharding import PartitionSpec as P
 
 HEAD = 128
+
+
+def split_up(shard, dim, peers):
+    before, after = (shard.shape[:dim], shard.shape[dim + 1 :])
+    return jnp.moveaxis(shard.reshape(*before, peers, -1, *after), dim, 0)
+
+
+def joined_along(pieces, dim):
+    pieces = jnp.moveaxis(pieces, 0, dim)
+    lengths = pieces.shape
+    return pieces.reshape(*lengths[:dim], lengths[dim] * lengths[dim + 1], *lengths[dim + 2 :])
 
 
 def shifted(value, axis, steps):
@@ -38,7 +49,14 @@
         local_rows,
         preferred_element_type=jnp.float32,
     ).astype(jnp.bfloat16)
-    moved = lax.all_to_all(partial_cols, "shard", split_axis=1, concat_axis=2, tiled=True)
+    devices, mine = (lax.axis_size("shard"), lax.axis_index("shard"))
+    pieces = split_up(partial_cols, 1, devices)
+    done = [pieces[mine]]
+    for step in range(1, devices):
+        sent = pieces[mine ^ step]
+        done.append(lax.ppermute(sent, "shard", [(i, i ^ step) for i in range(devices)]))
+    pieces = jnp.stack(done)[mine ^ jnp.arange(devices)]
+    moved = joined_along(pieces, 2)
     input_grad = moved[:, :, :width][None]
     passed = shifted(input_grad, "section", -1)
     steps_tok = normed.shape[1] * normed.shape[2]

time: 223 us -> 215 us (0.964)
  blocking collectives: 108 us -> 0 us
  waiting for transfers between devices: 71.4 us -> 166 us
  starting transfers between devices: 1.4 us -> 5.85 us
    all_to_all x1 -> x0, blocking collectives: 108 us -> none  [per_device(): lax.all_to_all(partial_cols, 'shard', split_axis=1, concat_axis=2, tiled=...]
    ppermute x0 -> x3, waiting for transfers between devices: none -> 99.2 us  [per_device(): lax.ppermute(sent, 'shard', [(i, i ^ step) for i in range(devices)])]
    broadcast_in_dim x1 -> x0, local copies, waits for them, and re-layouts: 4.53 us -> none  [per_device(): input_grad = moved[:, :, :width][None]]
    psum x1, waiting for transfers between devices: 38.7 us -> 34.3 us  [per_device(): total = lax.psum(shard_round.astype(jnp.bfloat16), 'replica')]
    ppermute x0 -> x3, starting transfers between devices: none -> 4.45 us  [per_device(): lax.ppermute(sent, 'shard', [(i, i ^ step) for i in range(devices)])]
    transpose x0 -> x1, local copies, waits for them, and re-layouts: none -> 3.96 us  [joined_along(): pieces = jnp.moveaxis(pieces, 0, dim)]
    gather x0 -> x1, local copies, waits for them, and re-layouts: none -> 3.66 us  [per_device(): pieces = jnp.stack(done)[mine ^ jnp.arange(devices)]]
    all_to_all x1 -> x0, local copies, waits for them, and re-layouts: 2.94 us -> none  [per_device(): lax.all_to_all(partial_cols, 'shard', split_axis=1, concat_axis=2, tiled=...]
  transfers between devices with their start and end apart: 4 -> 7, of which waited for: 3 -> 5; matrix products, arithmetic and copies ran while one was open for 7% -> 9% of each run, Pallas kernels for 0% -> 0%
where the time goes in v1:
time: 215 us
  waiting for transfers between devices  166 us (77%)
  local copies, waits for them, and re-layouts  17.8 us (8%)
  between operations  13.9 us (6%)
  starting transfers between devices  5.85 us (3%)
  matrix products  5.74 us (3%)
  other arithmetic  5.56 us (3%)
    ppermute x3, waiting for transfers between devices, per_device(): lax.ppermute(sent, 'shard', [(i, i ^ step) for i in range(devices)])  99.2 us
    psum x1, waiting for transfers between devices, per_device(): total = lax.psum(shard_round.astype(jnp.bfloat16), 'replica')  34.3 us
    all_gather x1, waiting for transfers between devices, per_device(): lax.all_gather(key_grad, 'shard', axis=1, tiled=True)  27.5 us
    unnamed x6, local copies, waits for them, and re-layouts  6.36 us
    ppermute x1, waiting for transfers between devices, shifted(): lax.ppermute(value, axis, [(source, source + steps) for source in range(l...  5.04 us
    ppermute x3, starting transfers between devices, per_device(): lax.ppermute(sent, 'shard', [(i, i ^ step) for i in range(devices)])  4.45 us
  transfers between devices with their start and end apart: 7, of which 5 were waited for; matrix products, arithmetic and copies ran while one was open for 9% of the time, Pallas kernels for 0%

profile of v1, /device:TPU:0, one launch (start us, length us, event | category | flops | bytes accessed | tf_op | source)
XLA Modules:
  0.0 214.9 jit_solution(2565810114340745589)
XLA Ops:
  7.2 0.0 copy-start
  7.2 0.0 all-gather.2.cloned.1.call-start
  7.2 1.3 reshape.98
  8.5 0.7 convert_element_type.52
  9.2 0.1 broadcast_multiply_fusion
  9.3 0.5 fusion.6
  9.8 0.4 fusion.9
  10.2 0.5 add_convert_fusion
  10.7 0.2 mul.71
  10.9 0.9 mul.65
  11.8 1.3 mul.69
  13.0 1.8 fusion.3
  14.8 0.0 all-gather.2.cloned.1.call-update
  14.9 0.0 reduce-scatter.2.cloned.1.call-start
  14.9 0.0 copy-done
  14.9 3.2 %fusion = bf16[4096,512]{0,1:T(8,128)(2,1)} fusion(bf16[256,4096]{1,0:T(8,128)(2,1)S(1)} %bitcast.39, bf16[32,8,4,128]{3,2,1,0:T(4,128)(2,1)S(1)} %bitcast.43), kind=kOutput, calls=%fused_computation.2 | convolution fusion | flops 1075838976 | bytes 6553600 | tf_op jit(solution)/shard_map/dot_general | solution.py:68
  18.2 0.0 copy-start.1
  18.2 0.0 reduce-scatter.2.cloned.1.call-update
  18.2 0.0 all-reduce.2.cloned.1.call-start
  18.2 27.5 %all-gather.2.cloned.1.call-done = bf16[2,512,512]{2,1,0:T(8,128)(2,1)} async-done(((bf16[2,128,512]{2,1,0:T(8,128)(2,1)}), bf16[2,512,512]{2,1,0:T(8,128)(2,1)}) %all-gather.2.cloned.1.call-update) | async-done | bytes 1048592 | tf_op jit(solution)/shard_map/all_gather | solution.py:48
  45.7 0.0 copy-done.1
  45.7 2.5 %convolution_convert_fusion.1 = bf16[2,512,1024]{2,1,0:T(8,128)(2,1)S(1)} fusion(bf16[2,512,512]{2,1,0:T(8,128)(2,1)} %all-gather.2.cloned.1.call-done, bf16[1,1024,512]{2,1,0:T(8,128)(2,1)S(1)} %copy-done.1), kind=kOutput, calls=%fused_computation.4 | convolution fusion | flops 1074790400 | bytes 4194304 | tf_op jit(solution)/shard_map/mtk,dk->mtd/dot_general | solution.py:46
  48.2 0.2 dynamic-slice_bitcast_fusion.3
  48.5 1.9 collective-permute-start.2
  50.3 1.1 collective-permute-start.1
  51.4 1.5 collective-permute-start
  52.9 20.2 %collective-permute-done.2 = bf16[2,128,1024]{2,1,0:T(8,128)(2,1)S(1)} collective-permute-done((bf16[2,128,1024]{2,1,0:T(8,128)(2,1)S(1)}, bf16[2,128,1024]{2,1,0:T(8,128)(2,1)S(1)}, u32[]{:S(2)}, u32[]{:S(2)}) %collective-permute-start.2) | collective-permute-done | bytes 524320 | tf_op jit(solution)/shard_map/ppermute | solution.py:57
  73.1 79.0 %collective-permute-done.1 = bf16[2,128,1024]{2,1,0:T(8,128)(2,1)S(1)} collective-permute-done((bf16[2,128,1024]{2,1,0:T(8,128)(2,1)S(1)}, bf16[2,128,1024]{2,1,0:T(8,128)(2,1)S(1)}, u32[]{:S(2)}, u32[]{:S(2)}) %collective-permute-start.1) | collective-permute-done | bytes 524320 | tf_op jit(solution)/shard_map/ppermute | solution.py:57
  152.1 0.0 collective-permute-done
  152.1 1.6 pad_maximum_fusion
  153.7 3.7 %gather_fusion = bf16[4,2,128,1024]{3,2,1,0:T(8,128)(2,1)} fusion(bf16[4,2,128,1024]{3,2,1,0:T(8,128)(2,1)} %pad_maximum_fusion, s32[1024]{0:T(1024)S(1)} %pad_clamp_fusion), kind=kCustom, calls=%fused_computation | custom fusion | bytes 4194320 | tf_op jit(solution)/shard_map/gather | solution.py:58
  157.4 4.0 %copy.8 = bf16[2,128,4,1024]{1,3,2,0:T(8,128)(2,1)} copy(bf16[2,128,4,1024]{3,1,0,2:T(8,128)(2,1)} %bitcast.40) | data formatting | bytes 4194304 | tf_op jit(solution)/shard_map/transpose | solution.py:15
  161.3 1.3 collective-permute-start.3
  162.6 0.0 reduce-scatter.2.cloned.1.call-done
  162.7 0.0 all-reduce.2.cloned.1.call-update
  162.7 5.0 %collective-permute-done.3 = bf16[1,2,128,4096]{2,3,1,0:T(8,128)(2,1)} collective-permute-done((bf16[1,2,128,4096]{2,3,1,0:T(8,128)(2,1)}, bf16[1,2,128,4096]{2,3,1,0:T(8,128)(2,1)}, u32[]{:S(2)}, u32[]{:S(2)}) %collective-permute-start.3) | collective-permute-done | bytes 2097184 | tf_op jit(solution)/shard_map/ppermute | solution.py:23
  167.7 4.1 %copy.10 = bf16[1,2,128,4096]{3,2,1,0:T(8,128)(2,1)} copy(bf16[1,2,128,4096]{2,3,1,0:T(8,128)(2,1)} %collective-permute-done.3) | data formatting | bytes 4194304
  171.8 34.3 %all-reduce.2.cloned.1.call-done = bf16[1,1024,512]{1,2,0:T(8,128)(2,1)} async-done(((bf16[1,1024,512]{1,2,0:T(8,128)(2,1)}), bf16[1,1024,512]{1,2,0:T(8,128)(2,1)}) %all-reduce.2.cloned.1.call-update) | async-done | bytes 1048592 | tf_op jit(solution)/shard_map/psum | solution.py:76
  206.1 2.3 %copy.9 = bf16[1,1024,512]{2,1,0:T(8,128)(2,1)} copy(bf16[1,1024,512]{1,2,0:T(8,128)(2,1)} %all-reduce.2.cloned.1.call-done) | data formatting | bytes 2097152
  (3 shorter events, 0.0 us)
Async XLA Ops:
  7.2 7.7 %copy-start = (bf16[1,2,128,4096]{3,2,1,0:T(8,128)(2,1)S(1)}, bf16[1,2,128,4096]{3,2,1,0:T(8,128)(2,1)}, u32[]{:S(2)}) copy-start(bf16[1,2,128,4096]{3,2,1,0:T(8,128)(2,1)} %param.4) | copy-start | bytes 6291460
  7.2 38.5 %all-gather.2.cloned.1.call-start = ((), (), s32[]{:S(2)}) async-start(), calls=%async_computation.3 | async-start | bytes 1310720 | tf_op jit(solution)/shard_map/all_gather | solution.py:48
  14.9 147.8 %reduce-scatter.2.cloned.1.call-start = ((), (), s32[]{:S(2)}) async-start(), calls=%async_computation.1 | async-start | bytes 5242880 | tf_op jit(solution)/shard_map/reduce_scatter | solution.py:67
  18.2 27.6 %copy-start.1 = (bf16[1,1024,512]{2,1,0:T(8,128)(2,1)S(1)}, bf16[1,1024,512]{2,1,0:T(8,128)(2,1)}, u32[]{:S(2)}) copy-start(bf16[1,1024,512]{2,1,0:T(8,128)(2,1)} %param.7) | copy-start | bytes 3145732
  18.2 187.9 %all-reduce.2.cloned.1.call-start = ((), (), s32[]{:S(2)}) async-start(), calls=%async_computation.2 | async-start | bytes 2097152 | tf_op jit(solution)/shard_map/psum | solution.py:76
  48.5 24.6 %collective-permute-start.2 = (bf16[2,128,1024]{2,1,0:T(8,128)(2,1)S(1)}, bf16[2,128,1024]{2,1,0:T(8,128)(2,1)S(1)}, u32[]{:S(2)}, u32[]{:S(2)}) collective-permute-start(bf16[2,128,1024]{2,1,0:T(8,128)(2,1)S(1)} %get-tuple-element.11), channel_id=1, source_target_pairs={{0,6},{2,4},{4,2},{6,0},{1,7},{3,5},{5,3},{7,1},{8,14},{10,12},{12... | collective-permute-start | bytes 1572872 | tf_op jit(solution)/shard_map/ppermute | solution.py:57
  50.3 101.8 %collective-permute-start.1 = (bf16[2,128,1024]{2,1,0:T(8,128)(2,1)S(1)}, bf16[2,128,1024]{2,1,0:T(8,128)(2,1)S(1)}, u32[]{:S(2)}, u32[]{:S(2)}) collective-permute-start(bf16[2,128,1024]{2,1,0:T(8,128)(2,1)S(1)} %get-tuple-element.12), channel_id=1, source_target_pairs={{0,4},{2,6},{4,0},{6,2},{1,5},{3,7},{5,1},{7,3},{8,12},{10,14},{12... | collective-permute-start | bytes 1572872 | tf_op jit(solution)/shard_map/ppermute | solution.py:57
  51.4 100.7 %collective-permute-start = (bf16[2,128,1024]{2,1,0:T(8,128)(2,1)S(1)}, bf16[2,128,1024]{2,1,0:T(8,128)(2,1)S(1)}, u32[]{:S(2)}, u32[]{:S(2)}) collective-permute-start(bf16[2,128,1024]{2,1,0:T(8,128)(2,1)S(1)} %get-tuple-element.13), channel_id=1, source_target_pairs={{0,2},{2,0},{4,6},{6,4},{1,3},{3,1},{5,7},{7,5},{8,10},{10,8},{12,... | collective-permute-start | bytes 1572872 | tf_op jit(solution)/shard_map/ppermute | solution.py:57
  161.3 6.4 %collective-permute-start.3 = (bf16[1,2,128,4096]{2,3,1,0:T(8,128)(2,1)}, bf16[1,2,128,4096]{2,3,1,0:T(8,128)(2,1)}, u32[]{:S(2)}, u32[]{:S(2)}) collective-permute-start(bf16[1,2,128,4096]{2,3,1,0:T(8,128)(2,1)} %bitcast.41), channel_id=1, source_target_pairs={{8,0},{16,8},{24,16},{9,1},{17,9},{25,17},{10,2},{18,10},{26,18},{... | collective-permute-start | bytes 6291464 | tf_op jit(solution)/shard_map/ppermute | solution.py:23
Sparse Core Ops, SparseCore 0:
  15.0 30.6 all-gather.1
  48.0 110.3 reduce-scatter.1
  162.8 43.2 all-reduce.1
